TPU v7x, 512 devices: a whole 4x8x8 slice. The times are simulated.
512 devices in a mesh: row: 32 (over y_lo, x, core), col: 16 (over z, y_hi).
Axes of the slice: x: 4, y: 8 (y_hi: 2, y_lo: 4; y = y_hi * 4 + y_lo), z: 8, core: 2. Of those that a mesh axis runs over, the one named last changes fastest.
Arguments:
- features: bfloat16 [98304, 256], P(('row', 'col')), may hold values from -6 to 6
- weight: bfloat16 [256, 256], replicated, may hold values from -0.375 to 0.375
- tiles: bfloat16 [32, 16, 256, 64, 128], P('row', 'col'), may hold values from -0.0546875 to 0.0546875
- tile_rows: int32 [32, 16, 512], P('row', 'col'), may hold values from 0 to 47
- tile_cols: int32 [32, 16, 512], P('row', 'col'), may hold values from 0 to 95
- counts: int32 [32, 16], P('row', 'col'), may hold values from 128 to 512, as said below
Outputs:
- output: bfloat16 [98304, 256], P(('row', 'col'))
Inputs may be any that keep to these rules, and one draw needn't show every extreme that they name: `counts`: some grid cell has exactly 512 live slots.
All inputs are finite; a program needn't handle non-finite values.
Results may differ from a plain program's by a relative error of at most 0.0049.
Values may be sent and summed in bfloat16 or wider, within the bound.
No kernel may reach another device: no remote copies, remote signals or barrier semaphores. Data moves between devices by JAX's collectives and lax.ppermute only.
A program may use at most 64 MiB of HBM per device.

v0:
```python
import jax
import jax.numpy as jnp
from jax import lax
from jax.sharding import PartitionSpec as P

TILE = 64


def body(features, weight, tiles, tile_rows, tile_cols, counts):
    feature_width = weight.shape[1]
    product_rows = jnp.dot(features, weight, preferred_element_type=jnp.float32).astype(
        jnp.bfloat16
    )
    gathered = lax.all_gather(product_rows, "row", axis=0, tiled=True)
    column_table = gathered.reshape(gathered.shape[0] // TILE, TILE, feature_width)
    row_tiles = lax.axis_size("col") * features.shape[0] // TILE
    slot_count = tile_rows.shape[2]
    block_size = min(64, slot_count)
    half_block = block_size // 2
    passes = slot_count // block_size
    pair_list = tiles[0, 0]
    row_list = tile_rows[0, 0]
    col_list = tile_cols[0, 0]
    live_count = counts[0, 0]
    block_slots = jnp.arange(block_size, dtype=jnp.int32)

    def add_block(block_index, total):
        first = block_index * block_size
        pair_block = lax.dynamic_slice_in_dim(pair_list, block_index * half_block, half_block, 0)
        pair_block = pair_block.reshape(half_block, TILE, 2, TILE)
        row_block = lax.dynamic_slice_in_dim(row_list, first, block_size, 0)
        col_block = lax.dynamic_slice_in_dim(col_list, first, block_size, 0)
        picked = column_table[col_block].reshape(half_block, 2, TILE, feature_width)
        terms = jnp.einsum(
            "qajb,qjbf->qjaf", pair_block, picked, preferred_element_type=jnp.float32
        )
        terms = terms.reshape(block_size, TILE, feature_width)
        in_use = (first + block_slots < live_count).astype(jnp.float32)
        terms = terms * in_use[:, None, None]
        return total.at[row_block].add(terms)

    zero_total = jnp.zeros((row_tiles, TILE, feature_width), jnp.float32)
    total = lax.fori_loop(0, passes, add_block, zero_total)
    partial_value = total.reshape(row_tiles * TILE, feature_width)
    own_rows = lax.psum_scatter(partial_value, "col", scatter_dimension=0, tiled=True)
    return jnp.maximum(own_rows, 0.0).astype(jnp.bfloat16)


def solution(mesh):
    return jax.shard_map(
        body,
        mesh=mesh,
        in_specs=(
            P(("row", "col"), None),
            P(),
            P("row", "col", None, None, None),
            P("row", "col", None),
            P("row", "col", None),
            P("row", "col"),
        ),
        out_specs=P(("row", "col"), None),
        check_vma=False,
    )
```

profile of v0, /device:TPU:12, one launch (start us, length us, event | category | flops | bytes accessed | tf_op | source)
XLA Modules:
  0.0 513.0 jit_solution(17624238361777435077)
XLA Ops:
  6.5 0.9 copy-done
  7.4 1.7 convolution_convert_fusion
  9.2 67.9 %all-gather.2.cloned.1.call-done = bf16[6144,256]{1,0:T(8,128)(2,1)} async-done(((bf16[192,256]{1,0:T(8,128)(2,1)}), bf16[6144,256]{1,0:T(8,128)(2,1)}) %all-gather.2.cloned.1.call-update) | async-done | bytes 3145744 | tf_op jit(solution)/shard_map/all_gather | solution.py:14
  77.5 195.1 %while.14 = (s32[]{:T(128)}, f32[48,64,256]{2,1,0:T(8,128)S(1)}, s32[512]{0:T(512)}, bf16[256,64,128]{2,1,0:T(8,128)(2,1)}, s32[512]{0:T(512)}, /*index=5*/bf16[...) while((s32[]{:T(128)}, f32[48,64,256]{2,1,0:T(8,128)S(1)}, ...), condition=%wide.region_2.0_spmd.clone, body=%wide.region_0.0_spmd.clone.sunk | while | flops 136316496 | bytes 34085360 | solution.py:43
  77.5 0.7 compare_convert_fusion.2
  78.1 0.8 compare_select_fusion.3
  78.9 1.9 constant_dynamic-slice_fusion.2
  80.8 3.2 reshape.70
  84.0 3.9 gather_fusion
  87.9 2.6 fusion.12
  90.5 2.5 bitcast_multiply_fusion.2
  93.0 8.8 %scatter_fusion = f32[48,64,256]{2,1,0:T(8,128)S(1)} fusion(f32[48,64,256]{2,1,0:T(8,128)S(1)} %get-tuple-element.238, s32[64]{0:T(128)S(1)} %get-tuple-element.222, f32[64,64,256]{2,1,0:T(8,128)} %bitcast_multiply_fusion.2), kind=kCustom, calls=%fused_computation.1.clone.clone.1 | custom fusion | flops 1048576 | bytes 12583168 | tf_op jit(solution)/shard_map/while/body/eval_jaxpr/scatter-add | solution.py:40
  102.5 0.8 compare_select_fusion.3
  103.3 1.9 constant_dynamic-slice_fusion.2
  105.2 3.2 reshape.70
  108.4 3.9 gather_fusion
  112.3 2.6 fusion.12
  114.9 2.5 bitcast_multiply_fusion.2
  117.4 8.8 %scatter_fusion = f32[48,64,256]{2,1,0:T(8,128)S(1)} fusion(f32[48,64,256]{2,1,0:T(8,128)S(1)} %get-tuple-element.238, s32[64]{0:T(128)S(1)} %get-tuple-element.222, f32[64,64,256]{2,1,0:T(8,128)} %bitcast_multiply_fusion.2), kind=kCustom, calls=%fused_computation.1.clone.clone.1 | custom fusion | flops 1048576 | bytes 12583168 | tf_op jit(solution)/shard_map/while/body/eval_jaxpr/scatter-add | solution.py:40
  126.9 0.8 compare_select_fusion.3
  127.7 1.9 constant_dynamic-slice_fusion.2
  129.6 3.2 reshape.70
  132.8 3.9 gather_fusion
  136.7 2.6 fusion.12
  139.3 2.5 bitcast_multiply_fusion.2
  141.8 8.8 %scatter_fusion = f32[48,64,256]{2,1,0:T(8,128)S(1)} fusion(f32[48,64,256]{2,1,0:T(8,128)S(1)} %get-tuple-element.238, s32[64]{0:T(128)S(1)} %get-tuple-element.222, f32[64,64,256]{2,1,0:T(8,128)} %bitcast_multiply_fusion.2), kind=kCustom, calls=%fused_computation.1.clone.clone.1 | custom fusion | flops 1048576 | bytes 12583168 | tf_op jit(solution)/shard_map/while/body/eval_jaxpr/scatter-add | solution.py:40
  151.3 0.8 compare_select_fusion.3
  152.1 1.9 constant_dynamic-slice_fusion.2
  154.0 3.2 reshape.70
  157.2 3.9 gather_fusion
  161.1 2.6 fusion.12
  163.7 2.5 bitcast_multiply_fusion.2
  166.2 8.8 %scatter_fusion = f32[48,64,256]{2,1,0:T(8,128)S(1)} fusion(f32[48,64,256]{2,1,0:T(8,128)S(1)} %get-tuple-element.238, s32[64]{0:T(128)S(1)} %get-tuple-element.222, f32[64,64,256]{2,1,0:T(8,128)} %bitcast_multiply_fusion.2), kind=kCustom, calls=%fused_computation.1.clone.clone.1 | custom fusion | flops 1048576 | bytes 12583168 | tf_op jit(solution)/shard_map/while/body/eval_jaxpr/scatter-add | solution.py:40
  175.7 0.8 compare_select_fusion.3
  176.5 1.9 constant_dynamic-slice_fusion.2
  178.4 3.2 reshape.70
  181.6 3.9 gather_fusion
  185.4 2.6 fusion.12
  188.1 2.5 bitcast_multiply_fusion.2
  190.6 8.8 %scatter_fusion = f32[48,64,256]{2,1,0:T(8,128)S(1)} fusion(f32[48,64,256]{2,1,0:T(8,128)S(1)} %get-tuple-element.238, s32[64]{0:T(128)S(1)} %get-tuple-element.222, f32[64,64,256]{2,1,0:T(8,128)} %bitcast_multiply_fusion.2), kind=kCustom, calls=%fused_computation.1.clone.clone.1 | custom fusion | flops 1048576 | bytes 12583168 | tf_op jit(solution)/shard_map/while/body/eval_jaxpr/scatter-add | solution.py:40
  200.1 0.8 compare_select_fusion.3
  200.9 1.9 constant_dynamic-slice_fusion.2
  202.8 3.2 reshape.70
  205.9 3.9 gather_fusion
  209.8 2.6 fusion.12
  212.4 2.5 bitcast_multiply_fusion.2
  215.0 8.8 %scatter_fusion = f32[48,64,256]{2,1,0:T(8,128)S(1)} fusion(f32[48,64,256]{2,1,0:T(8,128)S(1)} %get-tuple-element.238, s32[64]{0:T(128)S(1)} %get-tuple-element.222, f32[64,64,256]{2,1,0:T(8,128)} %bitcast_multiply_fusion.2), kind=kCustom, calls=%fused_computation.1.clone.clone.1 | custom fusion | flops 1048576 | bytes 12583168 | tf_op jit(solution)/shard_map/while/body/eval_jaxpr/scatter-add | solution.py:40
  224.5 0.8 compare_select_fusion.3
  225.3 1.9 constant_dynamic-slice_fusion.2
  227.1 3.2 reshape.70
  230.3 3.9 gather_fusion
  234.2 2.6 fusion.12
  236.8 2.5 bitcast_multiply_fusion.2
  239.4 8.8 %scatter_fusion = f32[48,64,256]{2,1,0:T(8,128)S(1)} fusion(f32[48,64,256]{2,1,0:T(8,128)S(1)} %get-tuple-element.238, s32[64]{0:T(128)S(1)} %get-tuple-element.222, f32[64,64,256]{2,1,0:T(8,128)} %bitcast_multiply_fusion.2), kind=kCustom, calls=%fused_computation.1.clone.clone.1 | custom fusion | flops 1048576 | bytes 12583168 | tf_op jit(solution)/shard_map/while/body/eval_jaxpr/scatter-add | solution.py:40
  248.9 0.8 compare_select_fusion.3
  249.7 1.9 constant_dynamic-slice_fusion.2
  251.5 3.2 reshape.70
  254.7 3.9 gather_fusion
  258.6 2.6 fusion.12
  261.2 2.5 bitcast_multiply_fusion.2
  263.8 8.8 %scatter_fusion = f32[48,64,256]{2,1,0:T(8,128)S(1)} fusion(f32[48,64,256]{2,1,0:T(8,128)S(1)} %get-tuple-element.238, s32[64]{0:T(128)S(1)} %get-tuple-element.222, f32[64,64,256]{2,1,0:T(8,128)} %bitcast_multiply_fusion.2), kind=kCustom, calls=%fused_computation.1.clone.clone.1 | custom fusion | flops 1048576 | bytes 12583168 | tf_op jit(solution)/shard_map/while/body/eval_jaxpr/scatter-add | solution.py:40
  272.6 1.6 copy-done.1
  274.3 230.3 %reduce-scatter.2.cloned.1.call-done = f32[192,256]{1,0:T(8,128)} async-done(((f32[3072,256]{1,0:T(8,128)}), f32[192,256]{1,0:T(8,128)}) %reduce-scatter.2.cloned.1.call-update) | async-done | bytes 196624 | tf_op jit(solution)/shard_map/reduce_scatter | solution.py:45
  504.6 1.6 maximum_convert_fusion
  (22 shorter events, 5.0 us)
Async XLA Ops:
  6.5 0.9 copy-start
  6.5 70.6 %all-gather.2.cloned.1.call-start = ((), (), s32[]{:S(2)}) async-start(), calls=%async_computation.1 | async-start | bytes 3244032 | tf_op jit(solution)/shard_map/all_gather | solution.py:14
  9.2 495.4 %reduce-scatter.2.cloned.1.call-start = ((), (), s32[]{:S(2)}) async-start(), calls=%async_computation.2 | async-start | bytes 3342336 | tf_op jit(solution)/shard_map/reduce_scatter | solution.py:45
  272.6 1.6 copy-start.1
Sparse Core Ops, SparseCore 0:
  9.5 67.5 all-gather.1
  274.4 230.1 reduce-scatter.1
where the time goes:
time: 516 us; the launch traced here: 513 us
  waiting for transfers between devices  298 us (58%)
  other arithmetic  104 us (20%)
  local copies, waits for them, and re-layouts  74.5 us (14%)
  matrix products  22.6 us (4%)
  between operations  13.4 us (3%)
    reduce_scatter x1, waiting for transfers between devices, body(): lax.psum_scatter(partial_value, 'col', scatter_dimension=0, tiled=True)  230 us
    scatter-add x8, other arithmetic, add_block(): return total.at[row_block].add(terms)  70.4 us
    all_gather x1, waiting for transfers between devices, body(): gathered = lax.all_gather(product_rows, 'row', axis=0, tiled=True)  67.9 us
    gather x8, local copies, waits for them, and re-layouts, add_block(): picked = column_table[col_block].reshape(half_block, 2, TILE, feature_width)  31.2 us
    reshape x8, local copies, waits for them, and re-layouts, add_block(): pair_block = pair_block.reshape(half_block, TILE, 2, TILE)  25.5 us
    dot_general x8, matrix products, add_block(): jnp.einsum('qajb,qjbf->qjaf', pair_block, picked, preferred_element_type=...  20.8 us
    mul x8, other arithmetic, add_block(): terms = terms * in_use[:, None, None]  20.4 us
    dynamic_slice x8, local copies, waits for them, and re-layouts, add_block(): lax.dynamic_slice_in_dim(pair_list, block_index * half_block, half_block, 0)  14.9 us
  transfers between devices with their start and end apart: 2, of which 2 were waited for; matrix products, arithmetic and copies ran while one was open for 0% of the time, Pallas kernels for 0%

commit v1 on v0

--- a/solution.py
+++ b/solution.py
@@ -11,7 +11,8 @@
     product_rows = jnp.dot(features, weight, preferred_element_type=jnp.float32).astype(
         jnp.bfloat16
     )
-    gathered = lax.all_gather(product_rows, "row", axis=0, tiled=True)
+    sent = jnp.stack([product_rows] * lax.axis_size("row"))
+    gathered = jnp.concatenate(lax.all_to_all(sent, "row", 0, 0), axis=0)
     column_table = gathered.reshape(gathered.shape[0] // TILE, TILE, feature_width)
     row_tiles = lax.axis_size("col") * features.shape[0] // TILE
     slot_count = tile_rows.shape[2]

time: 516 us -> 531 us (1.029)
  the two profiles are of different devices: /device:TPU:12 before, /device:TPU:10 now
where the time goes in v1:
time: 531 us; the launch traced here: 529 us
  waiting for transfers between devices  301 us (57%)
  other arithmetic  104 us (20%)
  local copies, waits for them, and re-layouts  78.2 us (15%)
  matrix products  21.9 us (4%)
  between operations  13.4 us (3%)
  starting transfers between devices  9.61 us (2%)
    reduce_scatter x1, waiting for transfers between devices, body(): lax.psum_scatter(partial_value, 'col', scatter_dimension=0, tiled=True)  233 us
    scatter-add x8, other arithmetic, add_block(): return total.at[row_block].add(terms)  70.4 us
    all_to_all x1, waiting for transfers between devices, body(): gathered = jnp.concatenate(lax.all_to_all(sent, 'row', 0, 0), axis=0)  68.3 us
    gather x8, local copies, waits for them, and re-layouts, add_block(): picked = column_table[col_block].reshape(half_block, 2, TILE, feature_width)  31.2 us
    reshape x8, local copies, waits for them, and re-layouts, add_block(): pair_block = pair_block.reshape(half_block, TILE, 2, TILE)  25.5 us
    dot_general x8, matrix products, add_block(): jnp.einsum('qajb,qjbf->qjaf', pair_block, picked, preferred_element_type=...  20.8 us
    mul x8, other arithmetic, add_block(): terms = terms * in_use[:, None, None]  20.4 us
    dynamic_slice x8, local copies, waits for them, and re-layouts, add_block(): lax.dynamic_slice_in_dim(pair_list, block_index * half_block, half_block, 0)  14.9 us
  transfers between devices with their start and end apart: 2, of which 2 were waited for; matrix products, arithmetic and copies ran while one was open for 0% of the time, Pallas kernels for 0%

profile of v1, /device:TPU:10, one launch (start us, length us, event | category | flops | bytes accessed | tf_op | source)
XLA Modules:
  0.0 528.7 jit_solution(17663666225599215256)
XLA Ops:
  6.5 0.9 copy-done
  7.4 1.1 convolution_convert_fusion
  8.5 2.0 stack.2
  10.5 9.6 %all-to-all-start = ((bf16[32,192,256]{2,1,0:T(8,128)(2,1)}), bf16[32,192,256]{2,1,0:T(8,128)(2,1)S(1)}, u32[]{:S(2)}, u32[]{:S(2)}) async-start(bf16[32,192,256]{2,1,0:T(8,128)(2,1)} %stack.2), calls=%async_computation | async-start | bytes 6291456 | tf_op jit(solution)/shard_map/all_to_all | solution.py:15
  20.1 68.3 %all-to-all-done = bf16[32,192,256]{2,1,0:T(8,128)(2,1)S(1)} async-done(((bf16[32,192,256]{2,1,0:T(8,128)(2,1)}), bf16[32,192,256]{2,1,0:T(8,128)(2,1)S(1)}, u32[]{:S(2)}, u32[]{:S(2)}) %all-to-all-start) | async-done | bytes 3145760 | tf_op jit(solution)/shard_map/all_to_all | solution.py:15
  88.4 1.7 copy-done.2
  90.5 195.1 %while.14 = (s32[]{:T(128)}, f32[48,64,256]{2,1,0:T(8,128)S(1)}, s32[512]{0:T(512)}, bf16[256,64,128]{2,1,0:T(8,128)(2,1)}, s32[512]{0:T(512)}, /*index=5*/bf16[...) while((s32[]{:T(128)}, f32[48,64,256]{2,1,0:T(8,128)S(1)}, ...), condition=%wide.region_2.0_spmd.clone, body=%wide.region_0.0_spmd.clone.sunk | while | flops 136316496 | bytes 34085360 | solution.py:44
  91.2 0.8 compare_select_fusion.3
  92.0 1.9 constant_dynamic-slice_fusion.2
  93.8 3.2 reshape.68
  97.0 3.9 gather_fusion
  100.9 2.6 fusion.12
  103.5 2.5 bitcast_multiply_fusion.2
  106.1 8.8 %scatter_fusion = f32[48,64,256]{2,1,0:T(8,128)S(1)} fusion(f32[48,64,256]{2,1,0:T(8,128)S(1)} %get-tuple-element.238, s32[64]{0:T(128)S(1)} %get-tuple-element.222, f32[64,64,256]{2,1,0:T(8,128)} %bitcast_multiply_fusion.2), kind=kCustom, calls=%fused_computation.1.clone.clone.1 | custom fusion | flops 1048576 | bytes 12583168 | tf_op jit(solution)/shard_map/while/body/eval_jaxpr/scatter-add | solution.py:41
  115.6 0.8 compare_select_fusion.3
  116.4 1.9 constant_dynamic-slice_fusion.2
  118.2 3.2 reshape.68
  121.4 3.9 gather_fusion
  125.3 2.6 fusion.12
  127.9 2.5 bitcast_multiply_fusion.2
  130.5 8.8 %scatter_fusion = f32[48,64,256]{2,1,0:T(8,128)S(1)} fusion(f32[48,64,256]{2,1,0:T(8,128)S(1)} %get-tuple-element.238, s32[64]{0:T(128)S(1)} %get-tuple-element.222, f32[64,64,256]{2,1,0:T(8,128)} %bitcast_multiply_fusion.2), kind=kCustom, calls=%fused_computation.1.clone.clone.1 | custom fusion | flops 1048576 | bytes 12583168 | tf_op jit(solution)/shard_map/while/body/eval_jaxpr/scatter-add | solution.py:41
  140.0 0.8 compare_select_fusion.3
  140.8 1.9 constant_dynamic-slice_fusion.2
  142.6 3.2 reshape.68
  145.8 3.9 gather_fusion
  149.7 2.6 fusion.12
  152.3 2.5 bitcast_multiply_fusion.2
  154.9 8.8 %scatter_fusion = f32[48,64,256]{2,1,0:T(8,128)S(1)} fusion(f32[48,64,256]{2,1,0:T(8,128)S(1)} %get-tuple-element.238, s32[64]{0:T(128)S(1)} %get-tuple-element.222, f32[64,64,256]{2,1,0:T(8,128)} %bitcast_multiply_fusion.2), kind=kCustom, calls=%fused_computation.1.clone.clone.1 | custom fusion | flops 1048576 | bytes 12583168 | tf_op jit(solution)/shard_map/while/body/eval_jaxpr/scatter-add | solution.py:41
  164.4 0.8 compare_select_fusion.3
  165.1 1.9 constant_dynamic-slice_fusion.2
  167.0 3.2 reshape.68
  170.2 3.9 gather_fusion
  174.1 2.6 fusion.12
  176.7 2.5 bitcast_multiply_fusion.2
  179.2 8.8 %scatter_fusion = f32[48,64,256]{2,1,0:T(8,128)S(1)} fusion(f32[48,64,256]{2,1,0:T(8,128)S(1)} %get-tuple-element.238, s32[64]{0:T(128)S(1)} %get-tuple-element.222, f32[64,64,256]{2,1,0:T(8,128)} %bitcast_multiply_fusion.2), kind=kCustom, calls=%fused_computation.1.clone.clone.1 | custom fusion | flops 1048576 | bytes 12583168 | tf_op jit(solution)/shard_map/while/body/eval_jaxpr/scatter-add | solution.py:41
  188.7 0.8 compare_select_fusion.3
  189.5 1.9 constant_dynamic-slice_fusion.2
  191.4 3.2 reshape.68
  194.6 3.9 gather_fusion
  198.5 2.6 fusion.12
  201.1 2.5 bitcast_multiply_fusion.2
  203.6 8.8 %scatter_fusion = f32[48,64,256]{2,1,0:T(8,128)S(1)} fusion(f32[48,64,256]{2,1,0:T(8,128)S(1)} %get-tuple-element.238, s32[64]{0:T(128)S(1)} %get-tuple-element.222, f32[64,64,256]{2,1,0:T(8,128)} %bitcast_multiply_fusion.2), kind=kCustom, calls=%fused_computation.1.clone.clone.1 | custom fusion | flops 1048576 | bytes 12583168 | tf_op jit(solution)/shard_map/while/body/eval_jaxpr/scatter-add | solution.py:41
  213.1 0.8 compare_select_fusion.3
  213.9 1.9 constant_dynamic-slice_fusion.2
  215.8 3.2 reshape.68
  219.0 3.9 gather_fusion
  222.9 2.6 fusion.12
  225.5 2.5 bitcast_multiply_fusion.2
  228.0 8.8 %scatter_fusion = f32[48,64,256]{2,1,0:T(8,128)S(1)} fusion(f32[48,64,256]{2,1,0:T(8,128)S(1)} %get-tuple-element.238, s32[64]{0:T(128)S(1)} %get-tuple-element.222, f32[64,64,256]{2,1,0:T(8,128)} %bitcast_multiply_fusion.2), kind=kCustom, calls=%fused_computation.1.clone.clone.1 | custom fusion | flops 1048576 | bytes 12583168 | tf_op jit(solution)/shard_map/while/body/eval_jaxpr/scatter-add | solution.py:41
  238.3 1.9 constant_dynamic-slice_fusion.2
  240.2 3.2 reshape.68
  243.4 3.9 gather_fusion
  247.3 2.6 fusion.12
  249.9 2.5 bitcast_multiply_fusion.2
  252.4 8.8 %scatter_fusion = f32[48,64,256]{2,1,0:T(8,128)S(1)} fusion(f32[48,64,256]{2,1,0:T(8,128)S(1)} %get-tuple-element.238, s32[64]{0:T(128)S(1)} %get-tuple-element.222, f32[64,64,256]{2,1,0:T(8,128)} %bitcast_multiply_fusion.2), kind=kCustom, calls=%fused_computation.1.clone.clone.1 | custom fusion | flops 1048576 | bytes 12583168 | tf_op jit(solution)/shard_map/while/body/eval_jaxpr/scatter-add | solution.py:41
  262.7 1.9 constant_dynamic-slice_fusion.2
  264.6 3.2 reshape.68
  267.7 3.9 gather_fusion
  271.6 2.6 fusion.12
  274.2 2.5 bitcast_multiply_fusion.2
  276.8 8.8 %scatter_fusion = f32[48,64,256]{2,1,0:T(8,128)S(1)} fusion(f32[48,64,256]{2,1,0:T(8,128)S(1)} %get-tuple-element.238, s32[64]{0:T(128)S(1)} %get-tuple-element.222, f32[64,64,256]{2,1,0:T(8,128)} %bitcast_multiply_fusion.2), kind=kCustom, calls=%fused_computation.1.clone.clone.1 | custom fusion | flops 1048576 | bytes 12583168 | tf_op jit(solution)/shard_map/while/body/eval_jaxpr/scatter-add | solution.py:41
  285.6 1.6 copy-done.1
  287.3 233.0 %reduce-scatter.2.cloned.1.call-done = f32[192,256]{1,0:T(8,128)} async-done(((f32[3072,256]{1,0:T(8,128)}), f32[192,256]{1,0:T(8,128)}) %reduce-scatter.2.cloned.1.call-update) | async-done | bytes 196624 | tf_op jit(solution)/shard_map/reduce_scatter | solution.py:46
  520.3 1.6 maximum_convert_fusion
  (24 shorter events, 7.2 us)
Async XLA Ops:
  6.5 0.9 copy-start
  10.5 77.9 %all-to-all-start = ((bf16[32,192,256]{2,1,0:T(8,128)(2,1)}), bf16[32,192,256]{2,1,0:T(8,128)(2,1)S(1)}, u32[]{:S(2)}, u32[]{:S(2)}) async-start(bf16[32,192,256]{2,1,0:T(8,128)(2,1)} %stack.2), calls=%async_computation | async-start | bytes 6291456 | tf_op jit(solution)/shard_map/all_to_all | solution.py:15
  20.1 500.2 %reduce-scatter.2.cloned.1.call-start = ((), (), s32[]{:S(2)}) async-start(), calls=%async_computation.2 | async-start | bytes 3342336 | tf_op jit(solution)/shard_map/reduce_scatter | solution.py:46
  88.4 1.7 copy-start.2
  285.6 1.6 copy-start.1
Sparse Core Ops, SparseCore 0:
  287.4 232.8 reduce-scatter.1
